TPU v7x, 256 devices: a whole 4x4x8 slice. The times are simulated.
256 devices in a mesh: op: 16 (over y, z_hi), right: 16 (over z_lo, x, core).
Axes of the slice: x: 4, y: 4, z: 8 (z_hi: 4, z_lo: 2; z = z_hi * 2 + z_lo), core: 2. Of those that a mesh axis runs over, the one named last changes fastest.
Arguments:
- psi: float32 [768, 16384], P('op', 'right'), may hold values from -6 to 6
- left_env: float32 [32, 768, 768], P('op', 'right'), may hold values from -0.078125 to 0.078125
- right_env: float32 [32, 16384, 1024], P('op', 'right'), may hold values from -0.1875 to 0.1875
- sector_lengths: int32 [4], replicated, may hold values from 128 to 384, as said below
- op_map: int32 [32, 4], replicated, may hold values from 0 to 3
Outputs:
- h_psi: float32 [768, 16384], P('op', 'right')
Inputs may be any that keep to these rules, and one draw needn't show every extreme that they name: `sector_lengths`: one sector, at a position that varies between draws, holds 384 states; every other sector holds 128.
All inputs are finite; a program needn't handle non-finite values.
Results may differ from a plain program's by a relative error of at most 0.0003.
Values sent between devices are 32-bit elements; how exact they have to be, the bound alone decides.
A program may use at most 64 MiB of HBM per device.

v0:
```python
import jax
import jax.numpy as jnp
from jax import lax
from jax.sharding import PartitionSpec as P


def on_device(psi, left_env, right_env, sector_lengths, op_map):
    terms = left_env.shape[0]
    width = left_env.shape[2]
    ends = jnp.cumsum(sector_lengths)
    places = jnp.arange(width, dtype=jnp.int32)
    sector = jnp.sum((places[:, None] >= ends[None, :]).astype(jnp.int32), axis=1)
    local_map = lax.dynamic_slice_in_dim(op_map, lax.axis_index("op") * terms, terms, 0)
    count = sector_lengths.shape[0]
    onehot = (sector[:, None] == jnp.arange(count, dtype=jnp.int32)[None, :]).astype(jnp.int32)
    targets = jnp.sum(onehot[None, :, :] * local_map[:, None, :], axis=2)
    whole = lax.all_gather(psi, "op", axis=0, tiled=True)
    inner = jnp.einsum("ac,wbc->wab", whole, right_env, precision=lax.Precision.HIGHEST)
    keep = (sector[None, :, None] == targets[:, None, :]).astype(jnp.float32)
    masked = lax.all_gather(left_env, "right", axis=1, tiled=True) * keep
    summed = jnp.einsum("wra,wab->rb", masked, inner, precision=lax.Precision.HIGHEST)
    return lax.psum_scatter(summed, "op", scatter_dimension=0, tiled=True)


def solution(mesh):
    in_specs = (P("op", "right"), P("op", "right", None), P("op", "right", None), P(), P())
    out_specs = P("op", "right")
    return jax.shard_map(
        on_device, mesh=mesh, in_specs=in_specs, out_specs=out_specs, check_vma=False
    )
```

profile of v0, /device:TPU:2, one launch (start us, length us, event | category | flops | bytes accessed | tf_op | source)
XLA Modules:
  0.0 239.5 jit_solution(2700261651093496640)
XLA Ops:
  6.5 0.0 copy-start
  6.5 0.0 all-gather.5.cloned.1.call-start
  6.5 0.7 all-gather.5.cloned.1.call-update
  7.3 0.0 all-gather.3.cloned.1.call-start
  7.3 0.7 all-gather.3.cloned.1.call-update
  8.0 0.0 reduce-scatter.2.cloned.1.call-start
  8.1 0.8 reduce-window.8
  8.9 0.0 copy-done
  8.9 0.1 constant_dynamic-slice_fusion
  9.0 0.1 copy.7
  9.1 0.1 convert_reduce_fusion
  9.2 0.1 multiply_reduce_fusion
  9.2 71.2 %all-gather.5.cloned.1.call-done = f32[768,1024]{1,0:T(8,128)} async-done(((f32[48,1024]{1,0:T(8,128)}), f32[768,1024]{1,0:T(8,128)}) %all-gather.5.cloned.1.call-update) | async-done | bytes 3145744 | tf_op jit(solution)/shard_map/all_gather | solution.py:17
  80.5 24.4 %fusion.4 = f32[2,1024,768]{1,2,0:T(8,128)} fusion(f32[2,1024,1024]{2,1,0:T(8,128)} %param.7, f32[768,1024]{1,0:T(8,128)} %all-gather.5.cloned.1.call-done), kind=kOutput, calls=%fused_computation.4 | convolution fusion | flops 19327352832 | bytes 17825792 | tf_op jit(solution)/shard_map/ac,wbc->wab/dot_general | solution.py:18
  104.8 16.0 %all-gather.3.cloned.1.call-done = f32[2,768,768]{2,1,0:T(8,128)} async-done(((f32[2,48,768]{2,1,0:T(8,128)}), f32[2,768,768]{2,1,0:T(8,128)}) %all-gather.3.cloned.1.call-update) | async-done | bytes 4718608 | tf_op jit(solution)/shard_map/all_gather | solution.py:20
  120.9 19.9 %fusion.9 = f32[768,1024]{1,0:T(8,128)} fusion(f32[2,1024,768]{1,2,0:T(8,128)} %fusion.4, f32[2,768,768]{2,1,0:T(8,128)} %all-gather.3.cloned.1.call-done, s32[2,768]{1,0:T(2,128)S(1)} %multiply_reduce_fusion, s32[768]{0:T(1024)S(1)} %convert_reduce_fusion), kind=kOutput, calls=%fused_computation.9 | convolution fusion | flops 14497873920 | bytes 14164992 | tf_op jit(solution)/shard_map/wra,wab->rb/dot_general | solution.py:21
  140.7 0.0 reduce-scatter.2.cloned.1.call-update
  140.8 92.2 %reduce-scatter.2.cloned.1.call-done = f32[48,1024]{1,0:T(8,128)} async-done(((f32[768,1024]{1,0:T(8,128)}), f32[48,1024]{1,0:T(8,128)}) %reduce-scatter.2.cloned.1.call-update) | async-done | bytes 196624 | tf_op jit(solution)/shard_map/reduce_scatter | solution.py:22
  (1 shorter events, 0.0 us)
Async XLA Ops:
  6.5 2.4 copy-start
  6.5 73.9 %all-gather.5.cloned.1.call-start = ((), (), s32[]{:S(2)}) async-start(), calls=%async_computation.2 | async-start | bytes 3342336 | tf_op jit(solution)/shard_map/all_gather | solution.py:17
  7.3 113.6 %all-gather.3.cloned.1.call-start = ((), (), s32[]{:S(2)}) async-start(), calls=%async_computation.1 | async-start | bytes 5013504 | tf_op jit(solution)/shard_map/all_gather | solution.py:20
  8.0 224.9 %reduce-scatter.2.cloned.1.call-start = ((), (), s32[]{:S(2)}) async-start(), calls=%async_computation.3 | async-start | bytes 3342336 | tf_op jit(solution)/shard_map/reduce_scatter | solution.py:22
Sparse Core Ops, SparseCore 0:
  9.8 70.5 all-gather.4
  82.3 38.5 all-gather.2
  140.9 92.0 reduce-scatter.1
where the time goes:
time: 240 us; the launch traced here: 239 us
  waiting for transfers between devices  181 us (75%)
  matrix products  44.3 us (18%)
  between operations  13.1 us (5%)
    reduce_scatter x1, waiting for transfers between devices, on_device(): return lax.psum_scatter(summed, 'op', scatter_dimension=0, tiled=True)  92.2 us
    all_gather x1, waiting for transfers between devices, on_device(): whole = lax.all_gather(psi, 'op', axis=0, tiled=True)  71.2 us
    dot_general x1, matrix products, on_device(): jnp.einsum('ac,wbc->wab', whole, right_env, precision=lax.Precision.HIGHEST)  24.4 us
    dot_general x1, matrix products, on_device(): jnp.einsum('wra,wab->rb', masked, inner, precision=lax.Precision.HIGHEST)  19.9 us
    all_gather x1, waiting for transfers between devices, on_device(): masked = lax.all_gather(left_env, 'right', axis=1, tiled=True) * keep  16 us
  transfers between devices with their start and end apart: 3, of which 3 were waited for; matrix products, arithmetic and copies ran while one was open for 11% of the time, Pallas kernels for 0%

commit v1 on v0

--- a/solution.py
+++ b/solution.py
@@ -14,7 +14,9 @@
     count = sector_lengths.shape[0]
     onehot = (sector[:, None] == jnp.arange(count, dtype=jnp.int32)[None, :]).astype(jnp.int32)
     targets = jnp.sum(onehot[None, :, :] * local_map[:, None, :], axis=2)
-    whole = lax.all_gather(psi, "op", axis=0, tiled=True)
+    whole = jnp.concatenate(
+        lax.all_to_all(jnp.stack([psi] * lax.axis_size("op")), "op", 0, 0), axis=0
+    )
     inner = jnp.einsum("ac,wbc->wab", whole, right_env, precision=lax.Precision.HIGHEST)
     keep = (sector[None, :, None] == targets[:, None, :]).astype(jnp.float32)
     masked = lax.all_gather(left_env, "right", axis=1, tiled=True) * keep

time: 240 us -> 256 us (1.067)
  starting transfers between devices: 0.08 us -> 11.2 us
  waiting for transfers between devices: 181 us -> 184 us
  local copies, waits for them, and re-layouts: 0.17 us -> 3.16 us
    all_to_all x0 -> x1, waiting for transfers between devices: none -> 75.4 us  [on_device(): lax.all_to_all(jnp.stack([psi] * lax.axis_size('op')), 'op', 0, 0)]
    all_gather x1 -> x0, waiting for transfers between devices: 71.2 us -> none  [on_device(): whole = lax.all_gather(psi, 'op', axis=0, tiled=True)]
    all_gather x1, waiting for transfers between devices: 16 us -> 0.01 us  [on_device(): masked = lax.all_gather(left_env, 'right', axis=1, tiled=True) * keep]
    reduce_scatter x1, waiting for transfers between devices: 92.2 us -> 108 us  [on_device(): return lax.psum_scatter(summed, 'op', scatter_dimension=0, tiled=True)]
    all_to_all x0 -> x1, starting transfers between devices: none -> 11.2 us  [on_device(): lax.all_to_all(jnp.stack([psi] * lax.axis_size('op')), 'op', 0, 0)]
    another operation x0 -> x1, local copies, waits for them, and re-layouts: none -> 2.99 us  [on_device(): jnp.stack([psi] * lax.axis_size('op'))]
  transfers between devices with their start and end apart: 3 -> 3, of which waited for: 3 -> 2; matrix products, arithmetic and copies ran while one was open for 11% -> 11% of each run, Pallas kernels for 0% -> 0%
where the time goes in v1:
time: 256 us
  waiting for transfers between devices  184 us (72%)
  matrix products  44 us (17%)
  between operations  13.4 us (5%)
  starting transfers between devices  11.2 us (4%)
  local copies, waits for them, and re-layouts  3.16 us (1%)
    reduce_scatter x1, waiting for transfers between devices, on_device(): return lax.psum_scatter(summed, 'op', scatter_dimension=0, tiled=True)  108 us
    all_to_all x1, waiting for transfers between devices, on_device(): lax.all_to_all(jnp.stack([psi] * lax.axis_size('op')), 'op', 0, 0)  75.4 us
    dot_general x1, matrix products, on_device(): jnp.einsum('ac,wbc->wab', whole, right_env, precision=lax.Precision.HIGHEST)  24.1 us
    dot_general x1, matrix products, on_device(): jnp.einsum('wra,wab->rb', masked, inner, precision=lax.Precision.HIGHEST)  19.9 us
    all_to_all x1, starting transfers between devices, on_device(): lax.all_to_all(jnp.stack([psi] * lax.axis_size('op')), 'op', 0, 0)  11.2 us
  transfers between devices with their start and end apart: 3, of which 2 were waited for; matrix products, arithmetic and copies ran while one was open for 11% of the time, Pallas kernels for 0%

profile of v1, /device:TPU:2, one launch (start us, length us, event | category | flops | bytes accessed | tf_op | source)
XLA Modules:
  0.0 255.9 jit_solution(10345859354932936538)
XLA Ops:
  6.5 0.0 copy-start
  6.5 0.0 all-gather.2.cloned.1.call-start
  6.5 0.7 all-gather.2.cloned.1.call-update
  7.3 0.0 copy-start.1
  7.3 3.0 %stack.2 = f32[16,48,1024]{2,1,0:T(8,128)} broadcast(f32[48,1024]{1,0:T(8,128)} %param.5), dimensions={1,2} | broadcast | bytes 3342336 | tf_op jit(solution)/shard_map/stack | solution.py:18
  10.3 11.2 %all-to-all-start = ((f32[16,48,1024]{2,1,0:T(8,128)}), f32[16,48,1024]{2,1,0:T(8,128)S(1)}, u32[]{:S(2)}, u32[]{:S(2)}) async-start(f32[16,48,1024]{2,1,0:T(8,128)} %stack.2), calls=%async_computation | async-start | bytes 6291456 | tf_op jit(solution)/shard_map/all_to_all | solution.py:18
  21.5 0.0 reduce-scatter.2.cloned.1.call-start
  21.5 0.0 copy-done.1
  21.5 0.2 reduce-window.8
  21.7 0.0 copy-done
  21.7 0.1 constant_dynamic-slice_fusion
  21.8 0.1 copy.7
  21.9 0.1 convert_reduce_fusion
  22.0 0.1 multiply_reduce_fusion
  22.1 75.4 %all-to-all-done = f32[16,48,1024]{2,1,0:T(8,128)S(1)} async-done(((f32[16,48,1024]{2,1,0:T(8,128)}), f32[16,48,1024]{2,1,0:T(8,128)S(1)}, u32[]{:S(2)}, u32[]{:S(2)}) %all-to-all-start) | async-done | bytes 3145760 | tf_op jit(solution)/shard_map/all_to_all | solution.py:18
  97.4 24.1 %fusion.14 = f32[2,1024,768]{1,2,0:T(8,128)} fusion(f32[2,1024,1024]{2,1,0:T(8,128)} %param.7, f32[768,1024,1]{1,0,2:T(8,128)S(1)} %bitcast.14), kind=kOutput, calls=%fused_computation.15 | convolution fusion | flops 19327352832 | bytes 17825792 | tf_op jit(solution)/shard_map/ac,wbc->wab/dot_general | solution.py:20
  121.6 0.0 all-gather.2.cloned.1.call-done
  121.6 19.9 %fusion.7 = f32[768,1024]{1,0:T(8,128)} fusion(f32[2,1024,768]{1,2,0:T(8,128)} %fusion.14, f32[2,768,768]{2,1,0:T(8,128)} %all-gather.2.cloned.1.call-done, s32[2,768]{1,0:T(2,128)S(1)} %multiply_reduce_fusion, s32[768]{0:T(1024)S(1)} %convert_reduce_fusion), kind=kOutput, calls=%fused_computation.7 | convolution fusion | flops 14497873920 | bytes 14164992 | tf_op jit(solution)/shard_map/wra,wab->rb/dot_general | solution.py:23
  141.5 0.0 reduce-scatter.2.cloned.1.call-update
  141.5 107.6 %reduce-scatter.2.cloned.1.call-done = f32[48,1024]{1,0:T(8,128)} async-done(((f32[768,1024]{1,0:T(8,128)}), f32[48,1024]{1,0:T(8,128)}) %reduce-scatter.2.cloned.1.call-update) | async-done | bytes 196624 | tf_op jit(solution)/shard_map/reduce_scatter | solution.py:24
  (1 shorter events, 0.0 us)
Async XLA Ops:
  6.5 15.2 %copy-start = (s32[32,4]{0,1:T(4,128)S(1)}, s32[32,4]{0,1:T(4,128)}, u32[]{:S(2)}) copy-start(s32[32,4]{0,1:T(4,128)} %param.9) | copy-start | bytes 1540
  6.5 115.0 %all-gather.2.cloned.1.call-start = ((), (), s32[]{:S(2)}) async-start(), calls=%async_computation.2 | async-start | bytes 5013504 | tf_op jit(solution)/shard_map/all_gather | solution.py:22
  7.3 14.3 %copy-start.1 = (s32[4]{0:T(128)S(1)}, s32[4]{0:T(128)}, u32[]{:S(2)}) copy-start(s32[4]{0:T(128)} %param.8) | copy-start | bytes 52
  10.3 87.2 %all-to-all-start = ((f32[16,48,1024]{2,1,0:T(8,128)}), f32[16,48,1024]{2,1,0:T(8,128)S(1)}, u32[]{:S(2)}, u32[]{:S(2)}) async-start(f32[16,48,1024]{2,1,0:T(8,128)} %stack.2), calls=%async_computation | async-start | bytes 6291456 | tf_op jit(solution)/shard_map/all_to_all | solution.py:18
  21.5 227.6 %reduce-scatter.2.cloned.1.call-start = ((), (), s32[]{:S(2)}) async-start(), calls=%async_computation.3 | async-start | bytes 3342336 | tf_op jit(solution)/shard_map/reduce_scatter | solution.py:24
Sparse Core Ops, SparseCore 0:
  9.2 87.3 all-gather.1
  141.6 107.4 reduce-scatter.1
